TPU v7x, 256 devices: a whole 4x4x8 slice. The times are simulated.
256 devices in a mesh: dp: 8 (over y, core), expert: 32 (over x, z).
Axes of the slice: x: 4, y: 4, z: 8, core: 2. Of those that a mesh axis runs over, the one named last changes fastest.
Arguments:
- tokens: bfloat16 [32768, 2048], P(('dp', 'expert')), may hold values from -6 to 6
- expert_ids: int32 [32768, 2], P(('dp', 'expert')), may hold values from 0 to 31, all different within a row; in each aligned block of 128 rows (0 to 127, 128 to 255, ...) at most 12 rows name the same one
- upstream: bfloat16 [32768, 2048], P(('dp', 'expert')), may hold values from -6 to 6
- gain: float32 [2048], replicated, may hold values from 0.5 to 1.5
- router: bfloat16 [2048, 32], replicated, may hold values from -0.125 to 0.125
- gate_weight_matrix: bfloat16 [32, 2048, 1024], P('expert', 'dp'), may hold values from -0.125 to 0.125
- up_weight: bfloat16 [32, 2048, 1024], P('expert', 'dp'), may hold values from -0.125 to 0.125
- down_weight: bfloat16 [32, 1024, 2048], P('expert', None, 'dp'), may hold values from -0.1875 to 0.1875
Outputs:
- mixed: bfloat16 [32768, 2048], P(('dp', 'expert'))
- d_tokens: bfloat16 [32768, 2048], P(('dp', 'expert'))
- gate_weight_gradient: bfloat16 [32, 2048, 1024], P('expert', 'dp')
- up_weight_gradient: bfloat16 [32, 2048, 1024], P('expert', 'dp')
- down_weight_gradient: bfloat16 [32, 1024, 2048], P('expert', None, 'dp')
- d_router: float32 [2048, 32], replicated
- d_gain: float32 [2048], replicated
Inputs may be any that keep to these rules, and one draw needn't show every extreme that they name: `expert_ids`: the two experts of a token differ. Among the tokens of one device (aligned blocks of 128 rows) no expert is named more than 12 times, and in some block one expert is named exactly 12 times.
All inputs are finite; a program needn't handle non-finite values.
Results may differ from a plain program's by a relative error of at most 0.014.
Values may be sent and summed in bfloat16 or wider, within the bound.
No kernel may reach another device: no remote copies, remote signals or barrier semaphores. Data moves between devices by JAX's collectives and lax.ppermute only.
A program may use at most 128 MiB of HBM per device.

v0:
```python
import jax
import jax.numpy as jnp
from jax import lax
from jax.sharding import PartitionSpec as P

norm_eps = 1e-06


def slot_layout(expert_ids, experts, capacity):
    flattened = expert_ids.reshape(-1)
    onehot = (flattened[:, None] == jnp.arange(experts, dtype=jnp.int32)[None, :]).astype(jnp.int32)
    ranking = jnp.sum(jnp.cumsum(onehot, axis=0) * onehot, axis=1) - 1
    slot_ids = flattened * capacity + ranking
    sources = (
        jnp.zeros((experts * capacity,), jnp.int32)
        .at[slot_ids]
        .set(jnp.arange(flattened.shape[0], dtype=jnp.int32))
    )
    counts = jnp.sum(onehot, axis=0)
    slots_occupied = (jnp.arange(capacity, dtype=jnp.int32)[None, :] < counts[:, None]).reshape(-1)
    return (slot_ids, sources, slots_occupied)


def transposed_product(left, right):
    return lax.dot_general(
        left, right, (((1,), (1,)), ((), ())), preferred_element_type=jnp.float32
    )


def inner_product(left, right):
    return lax.dot_general(
        left, right, (((0,), (0,)), ((), ())), preferred_element_type=jnp.float32
    )


def on_device(
    tokens, expert_ids, upstream, gain, router, gate_weight_matrix, up_weight, down_weight
):
    experts = lax.axis_size("expert")
    tok_rows = tokens.shape[0]
    width = tokens.shape[1]
    feed = gate_weight_matrix.shape[2]
    capacity = 3 * tok_rows // experts
    source = tokens.astype(jnp.float32)
    inverse = lax.rsqrt(jnp.mean(source * source, axis=-1, keepdims=True) + norm_eps)
    unit_rows = source * inverse
    normed = (unit_rows * gain).astype(jnp.bfloat16)
    scores = jax.nn.sigmoid(jnp.dot(normed, router, preferred_element_type=jnp.float32))
    picked = expert_ids[:, :, None] == jnp.arange(experts, dtype=jnp.int32)[None, None, :]
    chosen = jnp.sum(jnp.where(picked, scores[:, None, :], 0.0), axis=2)
    total = jnp.sum(chosen, axis=1, keepdims=True)
    gates = chosen / total
    slot_ids, sources, slots_occupied = slot_layout(expert_ids, experts, capacity)
    slot_pairs = slot_ids.reshape(tok_rows, 2)
    send_rows = jnp.where(
        slots_occupied[:, None], normed[sources // 2], jnp.zeros((), jnp.bfloat16)
    )
    arrived = lax.all_to_all(
        send_rows.reshape(experts, capacity, width),
        "expert",
        split_axis=0,
        concat_axis=0,
        tiled=True,
    )
    expert_in = arrived.reshape(experts * capacity, width)
    pieces = (
        lax.all_gather(gate_weight_matrix, "dp", axis=1, tiled=True),
        lax.all_gather(up_weight, "dp", axis=1, tiled=True),
    )
    columns = expert_in
    pre_gate = jnp.dot(columns, pieces[0][0], preferred_element_type=jnp.float32)
    pre_up = jnp.dot(columns, pieces[1][0], preferred_element_type=jnp.float32)
    sigma = jax.nn.sigmoid(pre_gate)
    active = pre_gate * sigma
    hidden = (active * pre_up).astype(jnp.bfloat16)
    expert_out = jnp.dot(
        hidden,
        lax.all_gather(down_weight, "dp", axis=2, tiled=True)[0],
        preferred_element_type=jnp.float32,
    ).astype(jnp.bfloat16)
    returned = lax.all_to_all(
        expert_out.reshape(experts, capacity, width),
        "expert",
        split_axis=0,
        concat_axis=0,
        tiled=True,
    )
    outputs = returned.reshape(experts * capacity, width)[slot_pairs].astype(jnp.float32)
    combined = gates[:, :, None] * outputs
    mixed = (source + combined[:, 0] + combined[:, 1]).astype(jnp.bfloat16)
    cotangent = upstream.astype(jnp.float32)
    d_gates = jnp.sum(cotangent[:, None, :] * outputs, axis=2)
    weight_rows = gates.reshape(-1)[sources]
    d_send = jnp.where(
        slots_occupied[:, None], weight_rows[:, None] * cotangent[sources // 2], 0.0
    ).astype(jnp.bfloat16)
    d_arrived = lax.all_to_all(
        d_send.reshape(experts, capacity, width), "expert", split_axis=0, concat_axis=0, tiled=True
    )
    d_out = d_arrived.reshape(experts * capacity, width)
    columns = d_out
    d_hidden = transposed_product(columns, lax.all_gather(down_weight, "dp", axis=2, tiled=True)[0])
    d_pre_gate = (d_hidden * pre_up * sigma * (1.0 + pre_gate * (1.0 - sigma))).astype(jnp.bfloat16)
    d_pre_up = (d_hidden * active).astype(jnp.bfloat16)
    pieces = (
        lax.all_gather(gate_weight_matrix, "dp", axis=1, tiled=True),
        lax.all_gather(up_weight, "dp", axis=1, tiled=True),
    )
    block = transposed_product(d_pre_gate, pieces[0][0]) + transposed_product(
        d_pre_up, pieces[1][0]
    )
    d_rows = block.astype(jnp.bfloat16)
    d_back = lax.all_to_all(
        d_rows.reshape(experts, capacity, width), "expert", split_axis=0, concat_axis=0, tiled=True
    )
    d_parts = d_back.reshape(experts * capacity, width)[slot_pairs].astype(jnp.float32)
    grad_rows = lax.psum_scatter(
        jnp.concatenate(
            [
                inner_product(expert_in, d_pre_gate),
                inner_product(expert_in, d_pre_up),
                inner_product(d_out, hidden),
            ],
            axis=1,
        ).astype(jnp.bfloat16),
        "dp",
        scatter_dimension=0,
        tiled=True,
    ).astype(jnp.float32)
    gate_weight_gradient = grad_rows[:, :feed].astype(jnp.bfloat16)[None]
    up_weight_gradient = grad_rows[:, feed : 2 * feed].astype(jnp.bfloat16)[None]
    down_weight_gradient = grad_rows[:, 2 * feed :].T.astype(jnp.bfloat16)[None]
    blended = jnp.sum(gates * d_gates, axis=1, keepdims=True)
    d_chosen = (d_gates - blended) / total
    d_logit = d_chosen * chosen * (1.0 - chosen)
    d_logits = jnp.sum(jnp.where(picked, d_logit[:, :, None], 0.0), axis=1)
    router_float = router.astype(jnp.float32)
    d_normed = (
        d_parts[:, 0]
        + d_parts[:, 1]
        + jnp.dot(d_logits, router_float.T, precision=lax.Precision.HIGHEST)
    )
    d_unit = d_normed * gain
    inner = jnp.mean(d_unit * unit_rows, axis=-1, keepdims=True)
    d_tokens = (cotangent + inverse * (d_unit - unit_rows * inner)).astype(jnp.bfloat16)
    part_router = jnp.dot(normed.astype(jnp.float32).T, d_logits, precision=lax.Precision.HIGHEST)
    part_gain = jnp.sum(d_normed * unit_rows, axis=0)
    d_router, d_gain = lax.psum((part_router, part_gain), ("dp", "expert"))
    return (
        mixed,
        d_tokens,
        gate_weight_gradient,
        up_weight_gradient,
        down_weight_gradient,
        d_router,
        d_gain,
    )


def solution(mesh):
    return jax.shard_map(
        on_device,
        mesh=mesh,
        in_specs=(
            P(("dp", "expert"), None),
            P(("dp", "expert"), None),
            P(("dp", "expert"), None),
            P(),
            P(),
            P("expert", "dp", None),
            P("expert", "dp", None),
            P("expert", None, "dp"),
        ),
        out_specs=(
            P(("dp", "expert"), None),
            P(("dp", "expert"), None),
            P("expert", "dp", None),
            P("expert", "dp", None),
            P("expert", None, "dp"),
            P(),
            P(),
        ),
        check_vma=False,
    )
```

profile of v0, /device:TPU:2, one launch (start us, length us, event | category | flops | bytes accessed | tf_op | source)
XLA Modules:
  0.0 638.8 jit_solution(4836383149556349928)
XLA Ops:
  13.7 3.1 gather_fusion
  16.8 2.4 gather.20
  19.5 60.0 %all_to_all.20 = bf16[32,12,2048]{2,1,0:T(8,128)(2,1)S(1)} all-to-all(bf16[32,12,2048]{2,1,0:T(8,128)(2,1)S(1)} %broadcast_select_fusion), channel_id=1, replica_groups=mesh['dp'=8,'expert'=32] {'expert'}, dimensions={0} | all-to-all | bytes 3145728 | tf_op jit(solution)/shard_map/all_to_all | solution.py:58
  80.9 5.8 fusion.10
  86.6 5.9 multiply_convert_fusion.2
  92.6 31.3 %all-gather.8.cloned.1.call-done = bf16[1,1024,2048]{2,1,0:T(8,128)(2,1)} async-done(((bf16[1,1024,256]{2,1,0:T(8,128)(2,1)}), bf16[1,1024,2048]{2,1,0:T(8,128)(2,1)}) %all-gather.8.cloned.1.call-update) | async-done | bytes 4194320 | tf_op jit(solution)/shard_map/all_gather | solution.py:78
  123.9 4.2 fusion.14
  129.7 10.3 %all-to-all-start.1 = ((bf16[32,12,2048]{2,1,0:T(8,128)(2,1)}), bf16[32,12,2048]{2,1,0:T(8,128)(2,1)}, u32[]{:S(2)}, u32[]{:S(2)}) async-start(bf16[32,12,2048]{2,1,0:T(8,128)(2,1)} %reshape.197), calls=%async_computation.1 | async-start | bytes 4194304 | tf_op jit(solution)/shard_map/all_to_all | solution.py:81
  140.6 3.3 gather_fusion.3
  143.9 4.6 gather.24
  148.9 39.2 %all-to-all-done.1 = bf16[32,12,2048]{2,1,0:T(8,128)(2,1)} async-done(((bf16[32,12,2048]{2,1,0:T(8,128)(2,1)}), bf16[32,12,2048]{2,1,0:T(8,128)(2,1)}, u32[]{:S(2)}, u32[]{:S(2)}) %all-to-all-start.1) | async-done | bytes 1572896 | tf_op jit(solution)/shard_map/all_to_all | solution.py:81
  188.1 2.5 reshape.198
  190.6 2.4 gather_fusion.1
  193.0 3.4 reshape.257
  196.3 2.6 multiply_reduce_fusion
  199.3 2.8 gather_fusion.2
  202.2 2.6 select_convert_fusion
  204.9 57.8 %all_to_all.21 = bf16[32,12,2048]{2,1,0:T(8,128)(2,1)S(1)} all-to-all(bf16[32,12,2048]{2,1,0:T(8,128)(2,1)S(1)} %select_convert_fusion), channel_id=1, replica_groups=mesh['dp'=8,'expert'=32] {'expert'}, dimensions={0} | all-to-all | bytes 3145728 | tf_op jit(solution)/shard_map/all_to_all | solution.py:97
  264.0 4.1 convolution_convert_fusion
  268.3 2.3 multiply_convert_fusion.1
  270.6 2.4 convolution_convert_fusion.2
  273.0 2.4 convolution_convert_fusion.1
  275.4 21.4 %pad_maximum_fusion = bf16[2048,3072]{0,1:T(8,128)(2,1)} fusion(bf16[2048,1024]{0,1:T(8,128)(2,1)S(1)} %convolution_convert_fusion, bf16[2048,1024]{0,1:T(8,128)(2,1)S(1)} %convolution_convert_fusion.1, bf16[2048,1024]{0,1:T(8,128)(2,1)S(1)} %convolution_convert_fusion.2), kind=kLoop, calls=%fused_computation.6 | loop fusion | flops 37748736 | bytes 25165824 | tf_op jit(solution)/shard_map/concatenate | solution.py:118
  297.9 4.2 fusion.4
  305.5 7.8 %all-to-all-start.3 = ((bf16[32,12,2048]{2,1,0:T(8,128)(2,1)}), bf16[32,12,2048]{2,1,0:T(8,128)(2,1)}, u32[]{:S(2)}, u32[]{:S(2)}) async-start(bf16[32,12,2048]{2,1,0:T(8,128)(2,1)} %reshape.200), calls=%async_computation.3 | async-start | bytes 4194304 | tf_op jit(solution)/shard_map/all_to_all | solution.py:113
  314.4 2.6 copy_multiply_fusion
  317.0 43.3 %all-to-all-done.3 = bf16[32,12,2048]{2,1,0:T(8,128)(2,1)} async-done(((bf16[32,12,2048]{2,1,0:T(8,128)(2,1)}), bf16[32,12,2048]{2,1,0:T(8,128)(2,1)}, u32[]{:S(2)}, u32[]{:S(2)}) %all-to-all-start.3) | async-done | bytes 1572896 | tf_op jit(solution)/shard_map/all_to_all | solution.py:113
  360.3 2.7 reshape.201
  367.4 2.3 fusion.31
  369.7 74.9 %psum.15 = f32[2048]{0:T(1024)} all-reduce(f32[2048]{0:T(1024)S(1)} %get-tuple-element.35), channel_id=1, replica_groups=mesh['dp'=8,'expert'=32] {'dp','expert'}, use_global_device_ids=true, to_apply=%region_15.16 | all-reduce | flops 2048 | bytes 16384 | tf_op jit(solution)/shard_map/psum | solution.py:148
  444.7 2.7 fusion.30
  451.7 178.7 %all-reduce.2.cloned.1.call-done = f32[2048,32]{0,1:T(8,128)} async-done(((f32[2048,32]{0,1:T(8,128)}), f32[2048,32]{0,1:T(8,128)}) %all-reduce.2.cloned.1.call-update) | async-done | bytes 262160 | tf_op jit(solution)/shard_map/psum | solution.py:148
  (102 shorter events, 28.3 us)
Async XLA Ops:
  7.2 141.4 %copy-start = (bf16[2048,32]{0,1:T(8,128)(2,1)S(1)}, bf16[2048,32]{0,1:T(8,128)(2,1)}, u32[]{:S(2)}) copy-start(bf16[2048,32]{0,1:T(8,128)(2,1)} %param.12) | copy-start | bytes 393220
  7.2 6.1 copy-start.3
  7.2 6.3 copy-start.10
  7.2 73.7 %all-gather.4.cloned.1.call-start = ((), (), s32[]{:S(2)}) async-start(), calls=%async_computation.5 | async-start | bytes 4718592 | tf_op jit(solution)/shard_map/all_gather | solution.py:67
  7.9 78.7 %all-gather.6.cloned.1.call-start = ((), (), s32[]{:S(2)}) async-start(), calls=%async_computation.6 | async-start | bytes 4718592 | tf_op jit(solution)/shard_map/all_gather | solution.py:68
  8.7 115.2 %all-gather.8.cloned.1.call-start = ((), (), s32[]{:S(2)}) async-start(), calls=%async_computation.7 | async-start | bytes 4718592 | tf_op jit(solution)/shard_map/all_gather | solution.py:78
  80.9 5.8 copy-start.7
  129.7 10.8 %copy-start.5 = (bf16[128,2048]{1,0:T(8,128)(2,1)S(1)}, bf16[128,2048]{1,0:T(8,128)(2,1)}, u32[]{:S(2)}) copy-start(bf16[128,2048]{1,0:T(8,128)(2,1)} %param.10) | copy-start | bytes 1572868
  129.7 58.4 %all-to-all-start.1 = ((bf16[32,12,2048]{2,1,0:T(8,128)(2,1)}), bf16[32,12,2048]{2,1,0:T(8,128)(2,1)}, u32[]{:S(2)}, u32[]{:S(2)}) async-start(bf16[32,12,2048]{2,1,0:T(8,128)(2,1)} %reshape.197), calls=%async_computation.1 | async-start | bytes 4194304 | tf_op jit(solution)/shard_map/all_to_all | solution.py:81
  140.0 307.4 %reduce-scatter.2.cloned.1.call-start = ((), (), s32[]{:S(2)}) async-start(), calls=%async_computation.8 | async-start | bytes 14155776 | tf_op jit(solution)/shard_map/reduce_scatter | solution.py:117
  143.9 4.9 copy-start.11
  264.0 4.2 copy-start.9
  264.0 4.2 copy-start.13
  264.0 4.2 copy-start.18
  264.0 4.3 copy-start.19
  268.3 2.3 copy-start.8
  270.5 2.4 copy-start.14
  270.6 2.4 copy-start.16
  296.8 1.1 copy-start.17
  297.9 4.2 copy-start.12
  297.9 4.2 copy-start.15
  305.5 8.9 %copy-start.1 = (f32[128,2,2048]{2,1,0:T(2,128)S(1)}, f32[128,2,2048]{2,1,0:T(2,128)}, u32[]{:S(2)}) copy-start(f32[128,2,2048]{2,1,0:T(2,128)} %reshape.257) | copy-start | bytes 6291460
  305.5 54.9 %all-to-all-start.3 = ((bf16[32,12,2048]{2,1,0:T(8,128)(2,1)}), bf16[32,12,2048]{2,1,0:T(8,128)(2,1)}, u32[]{:S(2)}, u32[]{:S(2)}) async-start(bf16[32,12,2048]{2,1,0:T(8,128)(2,1)} %reshape.200), calls=%async_computation.3 | async-start | bytes 4194304 | tf_op jit(solution)/shard_map/all_to_all | solution.py:113
  313.3 317.1 %all-reduce.2.cloned.1.call-start = ((), (), s32[]{:S(2)}) async-start(), calls=%async_computation.9 | async-start | bytes 524288 | tf_op jit(solution)/shard_map/psum | solution.py:148
  365.8 1.7 copy-start.4
  367.4 77.3 %copy-start.2 = (f32[128,2,2048]{2,0,1:T(8,128)S(1)}, f32[128,2,2048]{2,0,1:T(8,128)}, u32[]{:S(2)}) copy-start(f32[128,2,2048]{2,0,1:T(8,128)} %copy_multiply_fusion) | copy-start | bytes 6291460
  367.4 77.3 %copy-start.6 = (bf16[128,2048]{1,0:T(8,128)(2,1)S(1)}, bf16[128,2048]{1,0:T(8,128)(2,1)}, u32[]{:S(2)}) copy-start(bf16[128,2048]{1,0:T(8,128)(2,1)} %param.10) | copy-start | bytes 1572868
Sparse Core Ops, SparseCore 0:
  9.9 37.5 all-gather.3
  49.3 34.5 all-gather.5
  85.8 38.0 all-gather.7
  296.9 73.3 reduce-scatter.1
  376.2 254.0 all-reduce.1
where the time goes:
time: 646 us; the launch traced here: 639 us
  waiting for transfers between devices  295 us (46%)
  blocking collectives  193 us (30%)
  local copies, waits for them, and re-layouts  48 us (7%)
  matrix products  36.7 us (6%)
  other arithmetic  33.7 us (5%)
  starting transfers between devices  18.6 us (3%)
  between operations  14.5 us (2%)
    psum x1, waiting for transfers between devices, on_device(): d_router, d_gain = lax.psum((part_router, part_gain), ('dp', 'expert'))  179 us
    psum x1, blocking collectives, on_device(): d_router, d_gain = lax.psum((part_router, part_gain), ('dp', 'expert'))  74.9 us
    all_to_all x1, blocking collectives, on_device(): lax.all_to_all(send_rows.reshape(experts, capacity, width), 'expert', spl...  60 us
    all_to_all x1, blocking collectives, on_device(): lax.all_to_all(d_send.reshape(experts, capacity, width), 'expert', split_...  57.8 us
    all_to_all x1, waiting for transfers between devices, on_device(): lax.all_to_all(d_rows.reshape(experts, capacity, width), 'expert', split_...  43.3 us
    all_to_all x1, waiting for transfers between devices, on_device(): lax.all_to_all(expert_out.reshape(experts, capacity, width), 'expert', sp...  39.2 us
    all_gather x1, waiting for transfers between devices, on_device(): lax.all_gather(down_weight, 'dp', axis=2, tiled=True)[0]  31.3 us
    concatenate x1, other arithmetic, on_device(): jnp.concatenate([inner_product(expert_in, d_pre_gate), inner_product(expe...  21.4 us
  transfers between devices with their start and end apart: 7, of which 4 were waited for; matrix products, arithmetic and copies ran while one was open for 9% of the time, Pallas kernels for 0%

commit v1 on v0

--- a/solution.py
+++ b/solution.py
@@ -145,7 +145,7 @@
     d_tokens = (cotangent + inverse * (d_unit - unit_rows * inner)).astype(jnp.bfloat16)
     part_router = jnp.dot(normed.astype(jnp.float32).T, d_logits, precision=lax.Precision.HIGHEST)
     part_gain = jnp.sum(d_normed * unit_rows, axis=0)
-    d_router, d_gain = lax.psum((part_router, part_gain), ("dp", "expert"))
+    d_router, d_gain = lax.psum(lax.psum((part_router, part_gain), "dp"), "expert")
     return (
         mixed,
         d_tokens,

time: 646 us -> 536 us (0.83)
  waiting for transfers between devices: 295 us -> 226 us
  blocking collectives: 193 us -> 139 us
  starting transfers between devices: 18.6 us -> 29.3 us
    psum x1 -> x2, waiting for transfers between devices: 179 us -> 62.7 us  [the longest x1 62.7 us: on_device(): lax.psum(lax.psum((part_router, part_gain), 'dp'), 'expert')]
    all_to_all x1 -> x0, blocking collectives: 57.8 us -> none  [on_device(): lax.all_to_all(d_send.reshape(experts, capacity, width), 'expert', split_...]
    all_to_all x0 -> x1, waiting for transfers between devices: none -> 45.8 us  [on_device(): lax.all_to_all(d_send.reshape(experts, capacity, width), 'expert', split_...]
    all_to_all x0 -> x1, starting transfers between devices: none -> 8.84 us  [on_device(): lax.all_to_all(d_send.reshape(experts, capacity, width), 'expert', split_...]
    psum x1 -> x2, blocking collectives: 74.9 us -> 79 us  [the longest x1 65.9 us: on_device(): lax.psum(lax.psum((part_router, part_gain), 'dp'), 'expert')]
  transfers between devices with their start and end apart: 7 -> 9, of which waited for: 4 -> 5; matrix products, arithmetic and copies ran while one was open for 9% -> 18% of each run, Pallas kernels for 0% -> 0%
where the time goes in v1:
time: 536 us; the launch traced here: 528 us
  waiting for transfers between devices  226 us (42%)
  blocking collectives  139 us (26%)
  local copies, waits for them, and re-layouts  46.7 us (9%)
  matrix products  37 us (7%)
  other arithmetic  35 us (7%)
  starting transfers between devices  29.3 us (5%)
  between operations  14.8 us (3%)
    psum x1, blocking collectives, on_device(): lax.psum(lax.psum((part_router, part_gain), 'dp'), 'expert')  65.9 us
    psum x1, waiting for transfers between devices, on_device(): lax.psum(lax.psum((part_router, part_gain), 'dp'), 'expert')  62.7 us
    all_to_all x1, blocking collectives, on_device(): lax.all_to_all(send_rows.reshape(experts, capacity, width), 'expert', spl...  60 us
    all_to_all x1, waiting for transfers between devices, on_device(): lax.all_to_all(d_send.reshape(experts, capacity, width), 'expert', split_...  45.8 us
    all_to_all x1, waiting for transfers between devices, on_device(): lax.all_to_all(d_rows.reshape(experts, capacity, width), 'expert', split_...  44.6 us
    all_to_all x1, waiting for transfers between devices, on_device(): lax.all_to_all(expert_out.reshape(experts, capacity, width), 'expert', sp...  39.4 us
    all_gather x1, waiting for transfers between devices, on_device(): lax.all_gather(down_weight, 'dp', axis=2, tiled=True)[0]  31.2 us
    concatenate x1, other arithmetic, on_device(): jnp.concatenate([inner_product(expert_in, d_pre_gate), inner_product(expe...  21.4 us
  transfers between devices with their start and end apart: 9, of which 5 were waited for; matrix products, arithmetic and copies ran while one was open for 18% of the time, Pallas kernels for 0%

profile of v1, /device:TPU:2, one launch (start us, length us, event | category | flops | bytes accessed | tf_op | source)
XLA Modules:
  0.0 527.7 jit_solution(10643675346765394318)
XLA Ops:
  13.7 3.1 gather_fusion
  16.8 2.4 gather.20
  19.5 60.0 %all_to_all.20 = bf16[32,12,2048]{2,1,0:T(8,128)(2,1)S(1)} all-to-all(bf16[32,12,2048]{2,1,0:T(8,128)(2,1)S(1)} %broadcast_select_fusion), channel_id=1, replica_groups=mesh['dp'=8,'expert'=32] {'expert'}, dimensions={0} | all-to-all | bytes 3145728 | tf_op jit(solution)/shard_map/all_to_all | solution.py:58
  80.9 5.8 %fusion.10 = f32[384,1024]{1,0:T(8,128)} fusion(bf16[384,2048]{1,0:T(8,128)(2,1)} %reshape.196, bf16[1,2048,1024]{2,1,0:T(8,128)(2,1)} %all-gather.4.cloned.1.call-done), kind=kOutput, calls=%fused_computation.17 | convolution fusion | flops 1610612736 | bytes 7340032 | tf_op jit(solution)/shard_map/dot_general | solution.py:71
  86.6 6.0 %multiply_convert_fusion.2 = (bf16[384,1024]{1,0:T(8,128)(2,1)}, f32[384,1024]{1,0:T(8,128)}) fusion(f32[384,1024]{1,0:T(8,128)} %fusion.10, bf16[384,2048]{1,0:T(8,128)(2,1)S(1)} %copy-done.7, bf16[1,2048,1024]{2,1,0:T(8,128)(2,1)} %all-gather.6.cloned.1.call-done), kind=kOutput, calls=%fused_computation.31 | convolution fusion | flops 1612972032 | bytes 9699328 | tf_op jit(solution)/shard_map/dot_general | solution.py:72
  92.6 31.2 %all-gather.8.cloned.1.call-done = bf16[1,1024,2048]{2,1,0:T(8,128)(2,1)} async-done(((bf16[1,1024,256]{2,1,0:T(8,128)(2,1)}), bf16[1,1024,2048]{2,1,0:T(8,128)(2,1)}) %all-gather.8.cloned.1.call-update) | async-done | bytes 4194320 | tf_op jit(solution)/shard_map/all_gather | solution.py:78
  123.9 4.2 fusion.14
  129.7 10.8 %all-to-all-start.1 = ((bf16[32,12,2048]{2,1,0:T(8,128)(2,1)}), bf16[32,12,2048]{2,1,0:T(8,128)(2,1)}, u32[]{:S(2)}, u32[]{:S(2)}) async-start(bf16[32,12,2048]{2,1,0:T(8,128)(2,1)} %reshape.197), calls=%async_computation.1 | async-start | bytes 4194304 | tf_op jit(solution)/shard_map/all_to_all | solution.py:81
  140.7 3.3 gather_fusion.3
  144.0 4.6 gather.24
  148.9 39.4 %all-to-all-done.1 = bf16[32,12,2048]{2,1,0:T(8,128)(2,1)} async-done(((bf16[32,12,2048]{2,1,0:T(8,128)(2,1)}), bf16[32,12,2048]{2,1,0:T(8,128)(2,1)}, u32[]{:S(2)}, u32[]{:S(2)}) %all-to-all-start.1) | async-done | bytes 1572896 | tf_op jit(solution)/shard_map/all_to_all | solution.py:81
  188.3 2.5 reshape.198
  193.2 3.4 reshape.257
  196.6 2.6 multiply_reduce_fusion
  199.5 2.8 gather_fusion.2
  202.5 4.0 select_convert_fusion
  206.5 8.8 %all-to-all-start.2 = ((bf16[32,12,2048]{2,1,0:T(8,128)(2,1)}), bf16[32,12,2048]{2,1,0:T(8,128)(2,1)S(1)}, u32[]{:S(2)}, u32[]{:S(2)}) async-start(bf16[32,12,2048]{2,1,0:T(8,128)(2,1)} %select_convert_fusion), calls=%async_computation.2 | async-start | bytes 4194304 | tf_op jit(solution)/shard_map/all_to_all | solution.py:97
  217.0 45.8 %all-to-all-done.2 = bf16[32,12,2048]{2,1,0:T(8,128)(2,1)S(1)} async-done(((bf16[32,12,2048]{2,1,0:T(8,128)(2,1)}), bf16[32,12,2048]{2,1,0:T(8,128)(2,1)S(1)}, u32[]{:S(2)}, u32[]{:S(2)}) %all-to-all-start.2) | async-done | bytes 1572896 | tf_op jit(solution)/shard_map/all_to_all | solution.py:97
  264.2 4.1 convolution_convert_fusion
  270.7 2.4 convolution_convert_fusion.2
  273.2 2.4 convolution_convert_fusion.1
  275.6 21.4 %pad_maximum_fusion = bf16[2048,3072]{0,1:T(8,128)(2,1)} fusion(bf16[2048,1024]{0,1:T(8,128)(2,1)S(1)} %convolution_convert_fusion, bf16[2048,1024]{0,1:T(8,128)(2,1)S(1)} %convolution_convert_fusion.1, bf16[2048,1024]{0,1:T(8,128)(2,1)S(1)} %convolution_convert_fusion.2), kind=kLoop, calls=%fused_computation.6 | loop fusion | flops 37748736 | bytes 25165824 | tf_op jit(solution)/shard_map/concatenate | solution.py:118
  297.0 4.2 fusion.4
  304.6 8.9 %all-to-all-start.3 = ((bf16[32,12,2048]{2,1,0:T(8,128)(2,1)}), bf16[32,12,2048]{2,1,0:T(8,128)(2,1)}, u32[]{:S(2)}, u32[]{:S(2)}) async-start(bf16[32,12,2048]{2,1,0:T(8,128)(2,1)} %reshape.200), calls=%async_computation.3 | async-start | bytes 4194304 | tf_op jit(solution)/shard_map/all_to_all | solution.py:113
  313.5 2.6 copy_multiply_fusion
  316.2 44.6 %all-to-all-done.3 = bf16[32,12,2048]{2,1,0:T(8,128)(2,1)} async-done(((bf16[32,12,2048]{2,1,0:T(8,128)(2,1)}), bf16[32,12,2048]{2,1,0:T(8,128)(2,1)}, u32[]{:S(2)}, u32[]{:S(2)}) %all-to-all-start.3) | async-done | bytes 1572896 | tf_op jit(solution)/shard_map/all_to_all | solution.py:113
  360.8 2.7 reshape.201
  367.9 2.4 fusion.31
  370.3 13.1 %psum.30 = f32[2048]{0:T(1024)S(1)} all-reduce(f32[2048]{0:T(1024)S(1)} %get-tuple-element.35), channel_id=1, replica_groups=mesh['dp'=8,'expert'=32] {'dp'}, use_global_device_ids=true, to_apply=%region_16.17 | all-reduce | flops 2048 | bytes 16384 | tf_op jit(solution)/shard_map/psum | solution.py:148
  383.3 65.9 %psum.31 = f32[2048]{0:T(1024)} all-reduce(f32[2048]{0:T(1024)S(1)} %psum.30), channel_id=1, replica_groups=mesh['dp'=8,'expert'=32] {'expert'}, use_global_device_ids=true, to_apply=%region_17.18 | all-reduce | flops 2048 | bytes 16384 | tf_op jit(solution)/shard_map/psum | solution.py:148
  449.3 2.7 fusion.30
  456.2 62.7 %all-reduce.5.cloned.1.call-done = f32[2048,32]{0,1:T(8,128)} async-done(((f32[2048,32]{0,1:T(8,128)}), f32[2048,32]{0,1:T(8,128)}) %all-reduce.5.cloned.1.call-update) | async-done | bytes 262160 | tf_op jit(solution)/shard_map/psum | solution.py:148
  (99 shorter events, 32.1 us)
Async XLA Ops:
  7.2 141.4 %copy-start = (bf16[2048,32]{0,1:T(8,128)(2,1)S(1)}, bf16[2048,32]{0,1:T(8,128)(2,1)}, u32[]{:S(2)}) copy-start(bf16[2048,32]{0,1:T(8,128)(2,1)} %param.12) | copy-start | bytes 393220
  7.2 6.1 %copy-start.3 = (bf16[128,2048]{1,0:T(8,128)(2,1)S(1)}, bf16[128,2048]{1,0:T(8,128)(2,1)}, u32[]{:S(2)}) copy-start(bf16[128,2048]{1,0:T(8,128)(2,1)} %param.8) | copy-start | bytes 1572868
  7.2 6.3 %copy-start.10 = (f32[2048]{0:T(1024)S(1)}, f32[2048]{0:T(1024)}, u32[]{:S(2)}) copy-start(f32[2048]{0:T(1024)} %param.11) | copy-start | bytes 24580
  7.2 73.7 %all-gather.4.cloned.1.call-start = ((), (), s32[]{:S(2)}) async-start(), calls=%async_computation.5 | async-start | bytes 4718592 | tf_op jit(solution)/shard_map/all_gather | solution.py:67
  7.9 78.7 %all-gather.6.cloned.1.call-start = ((), (), s32[]{:S(2)}) async-start(), calls=%async_computation.6 | async-start | bytes 4718592 | tf_op jit(solution)/shard_map/all_gather | solution.py:68
  8.7 115.2 %all-gather.8.cloned.1.call-start = ((), (), s32[]{:S(2)}) async-start(), calls=%async_computation.7 | async-start | bytes 4718592 | tf_op jit(solution)/shard_map/all_gather | solution.py:78
  80.9 5.8 %copy-start.7 = (bf16[384,2048]{1,0:T(8,128)(2,1)S(1)}, bf16[384,2048]{1,0:T(8,128)(2,1)}, u32[]{:S(2)}) copy-start(bf16[384,2048]{1,0:T(8,128)(2,1)} %reshape.196) | copy-start | bytes 4718596
  129.7 11.0 %copy-start.5 = (bf16[128,2048]{1,0:T(8,128)(2,1)S(1)}, bf16[128,2048]{1,0:T(8,128)(2,1)}, u32[]{:S(2)}) copy-start(bf16[128,2048]{1,0:T(8,128)(2,1)} %param.10) | copy-start | bytes 1572868
  129.7 58.7 %all-to-all-start.1 = ((bf16[32,12,2048]{2,1,0:T(8,128)(2,1)}), bf16[32,12,2048]{2,1,0:T(8,128)(2,1)}, u32[]{:S(2)}, u32[]{:S(2)}) async-start(bf16[32,12,2048]{2,1,0:T(8,128)(2,1)} %reshape.197), calls=%async_computation.1 | async-start | bytes 4194304 | tf_op jit(solution)/shard_map/all_to_all | solution.py:81
  144.0 4.9 copy-start.11
  206.5 56.4 %all-to-all-start.2 = ((bf16[32,12,2048]{2,1,0:T(8,128)(2,1)}), bf16[32,12,2048]{2,1,0:T(8,128)(2,1)S(1)}, u32[]{:S(2)}, u32[]{:S(2)}) async-start(bf16[32,12,2048]{2,1,0:T(8,128)(2,1)} %select_convert_fusion), calls=%async_computation.2 | async-start | bytes 4194304 | tf_op jit(solution)/shard_map/all_to_all | solution.py:97
  215.3 100.8 %all-reduce.3.cloned.1.call-start = ((), (), s32[]{:S(2)}) async-start(), calls=%async_computation.9 | async-start | bytes 524288 | tf_op jit(solution)/shard_map/psum | solution.py:148
  216.5 235.5 %reduce-scatter.2.cloned.1.call-start = ((), (), s32[]{:S(2)}) async-start(), calls=%async_computation.8 | async-start | bytes 14155776 | tf_op jit(solution)/shard_map/reduce_scatter | solution.py:117
  264.2 4.2 copy-start.9
  264.2 4.2 copy-start.13
  264.2 4.2 copy-start.14
  264.2 4.3 copy-start.15
  268.4 2.3 copy-start.8
  297.0 4.2 copy-start.12
  304.6 8.9 %copy-start.1 = (f32[128,2,2048]{2,1,0:T(2,128)S(1)}, f32[128,2,2048]{2,1,0:T(2,128)}, u32[]{:S(2)}) copy-start(f32[128,2,2048]{2,1,0:T(2,128)} %reshape.257) | copy-start | bytes 6291460
  304.6 56.2 %all-to-all-start.3 = ((bf16[32,12,2048]{2,1,0:T(8,128)(2,1)}), bf16[32,12,2048]{2,1,0:T(8,128)(2,1)}, u32[]{:S(2)}, u32[]{:S(2)}) async-start(bf16[32,12,2048]{2,1,0:T(8,128)(2,1)} %reshape.200), calls=%async_computation.3 | async-start | bytes 4194304 | tf_op jit(solution)/shard_map/all_to_all | solution.py:113
  313.5 205.5 %all-reduce.5.cloned.1.call-start = ((), (), s32[]{:S(2)}) async-start(), calls=%async_computation.10 | async-start | bytes 524288 | tf_op jit(solution)/shard_map/psum | solution.py:148
  366.2 1.7 copy-start.4
  367.8 81.4 %copy-start.2 = (f32[128,2,2048]{2,0,1:T(8,128)S(1)}, f32[128,2,2048]{2,0,1:T(8,128)}, u32[]{:S(2)}) copy-start(f32[128,2,2048]{2,0,1:T(8,128)} %copy_multiply_fusion) | copy-start | bytes 6291460
  367.8 81.4 %copy-start.6 = (bf16[128,2048]{1,0:T(8,128)(2,1)S(1)}, bf16[128,2048]{1,0:T(8,128)(2,1)}, u32[]{:S(2)}) copy-start(bf16[128,2048]{1,0:T(8,128)(2,1)} %param.10) | copy-start | bytes 1572868
Sparse Core Ops, SparseCore 0:
  9.9 37.5 all-gather.3
  49.3 34.5 all-gather.5
  85.8 38.0 all-gather.7
  218.7 66.7 all-reduce.2
  297.1 74.4 reduce-scatter.1
  374.9 143.9 all-reduce.4
